TPU v7x, 128 devices: a whole 4x4x4 slice. The times are simulated.
128 devices in a mesh: tm: 32 (over z, y, core), rep: 4 (over x).
Axes of the slice: x: 4, y: 4, z: 4, core: 2. Of those that a mesh axis runs over, the one named last changes fastest.
Arguments:
- transitions: float32 [128, 512, 512], P(('rep', 'tm')), parts along dimension 0, may hold values from -1 to 1, as said below
- cond_covs: float32 [128, 512, 512], P(('rep', 'tm')), parts along dimension 0, may hold values from -40 to 40, as said below
- transition_est: float32 [2048, 512], P('rep'), parts along dimension 0, may hold values from -0.25 to 0.25
Outputs:
- cov_blocks: float32 [128, 512, 512], P(('rep', 'tm')), parts along dimension 0
- transition_grad: float32 [2048, 512], P('rep'), parts along dimension 0
There are 4 independent parts, one for each index of `rep`. A program takes and returns all parts, laid end to end along the dimension named above; each array names one. Nothing has to cross between parts.
Inputs may be any that keep to these rules, and one draw needn't show every extreme that they name: `transitions`: every block has spectral norm below one. `cond_covs`: every block is symmetric and positive definite.
All inputs are finite; a program needn't handle non-finite values.
Results may differ from a plain program's by a relative error of at most 0.00017.
Values sent between devices are 32-bit elements; how exact they have to be, the bound alone decides.
No kernel may reach another device: no remote copies, remote signals or barrier semaphores. Data moves between devices by JAX's collectives and lax.ppermute only.
A program may use at most 192 MiB of HBM per device.

v0:
```python
import jax
import jax.numpy as jnp
from jax import lax
from jax.sharding import PartitionSpec as P

highest = lax.Precision.HIGHEST


def entering(part, axis, combine, identity):
    count = lax.axis_size(axis)
    place = lax.axis_index(axis)
    ahead = count - 1 - place
    gathered = jax.tree.map(lambda a: lax.all_gather(a, axis), part)
    state = jax.tree.map(lambda a, e: jnp.zeros_like(a) + jnp.asarray(e, a.dtype), part, identity)

    def one(step, state):
        source = count - 1 - step
        return combine(
            state, jax.tree.map(lambda a: lax.dynamic_index_in_dim(a, source, 0, False), gathered)
        )

    return lax.fori_loop(0, ahead, one, state)


def times_transposed(left, right):
    return lax.dot_general(
        left, right, (((1,), (1,)), ((), ())), precision=highest, preferred_element_type=jnp.float32
    )


def product(left, right):
    return jnp.dot(left, right, precision=highest, preferred_element_type=jnp.float32)


def compose(earlier, latter):
    gain_first, noise_first = earlier
    gain_second, second_noise = latter
    combined_gain = product(gain_second, gain_first)
    combined_noise = product(gain_second, times_transposed(noise_first, gain_second)) + second_noise
    return (combined_gain, combined_noise)


def on_device(transitions, cond_covs, transition_est):
    blocks_here = transitions.shape[0]
    width = transitions.shape[1]
    devices = lax.axis_size("tm")
    total_blocks = blocks_here * devices
    position = lax.axis_index("tm")
    combined_gain = transitions[blocks_here - 1]
    combined_noise = cond_covs[blocks_here - 1]
    empty_block = jnp.zeros((width, width), jnp.float32)
    identity = jnp.eye(width, dtype=jnp.float32)
    prefix = entering((combined_gain, combined_noise), "tm", compose, (identity, empty_block))
    covariance = prefix[1]
    transition = transitions[0]
    previous_step_cross = times_transposed(covariance, transition)
    covariance = product(transition, previous_step_cross) + cond_covs[0]
    collected = [covariance]
    current_entry = jnp.where(position * blocks_here + 0 < total_blocks - 1, 1.0, 0.0).astype(
        jnp.float32
    )
    accumulated = current_entry * (previous_step_cross - product(transition_est, covariance))
    gradient = lax.psum(accumulated, "tm") / (total_blocks - 1)
    cov_blocks = jnp.stack(collected[::-1], axis=0)
    return (cov_blocks, gradient)


def solution(mesh):
    return jax.shard_map(
        on_device,
        mesh=mesh,
        in_specs=(P(("rep", "tm"), None, None), P(("rep", "tm"), None, None), P("rep", None)),
        out_specs=(P(("rep", "tm"), None, None), P("rep", None)),
        check_vma=False,
    )
```

profile of v0, /device:TPU:1, one launch (start us, length us, event | category | flops | bytes accessed | tf_op | source)
XLA Modules:
  0.0 565.4 jit_solution(15440725541577680220)
XLA Ops:
  11.3 116.7 %all-gather.3.cloned.1.call-done = f32[32,512,512]{2,1,0:T(8,128)} async-done(((f32[1,512,512]{2,1,0:T(8,128)}), f32[32,512,512]{2,1,0:T(8,128)}) %all-gather.3.cloned.1.call-update) | async-done | bytes 33554448 | tf_op jit(solution)/shard_map/all_gather | solution.py:13
  127.9 115.5 %all-gather.5.cloned.1.call-done = f32[32,512,512]{2,1,0:T(8,128)} async-done(((f32[1,512,512]{2,1,0:T(8,128)}), f32[32,512,512]{2,1,0:T(8,128)}) %all-gather.5.cloned.1.call-update) | async-done | bytes 33554448 | tf_op jit(solution)/shard_map/all_gather | solution.py:13
  243.5 196.2 %while.14 = (s32[]{:T(128)}, f32[512,512]{1,0:T(8,128)S(1)}, s32[]{:T(128)}, f32[32,512,512]{2,1,0:T(8,128)}, f32[32,512,512]{2,1,0:T(8,128)}, /*index=5*/s32[]{:T(128)}, s32[]{:T(128)}, s32[]{:T(128)}, s32[]{:T(128)}) while((s32[]{:T(128)}, f32[512,512]{1,0:T(8,128)S(1)}, s32[]{:T(128)}, f32[32,512,512]{2,1,0:T(8,128)}, ...), condition=%wide.region_1.2_spmd, body=%wide.region_0.1_spmd.sunk | while | flops 3221487616 | bytes 7341199 | solution.py:22
  246.6 3.4 convolution_add_fusion.2
  253.2 3.4 convolution_add_fusion.2
  259.7 3.4 convolution_add_fusion.2
  266.2 3.4 convolution_add_fusion.2
  272.8 3.4 convolution_add_fusion.2
  279.3 3.4 convolution_add_fusion.2
  285.8 3.4 convolution_add_fusion.2
  292.4 3.4 convolution_add_fusion.2
  298.9 3.4 convolution_add_fusion.2
  305.4 3.4 convolution_add_fusion.2
  312.0 3.4 convolution_add_fusion.2
  318.5 3.4 convolution_add_fusion.2
  325.0 3.4 convolution_add_fusion.2
  331.6 3.4 convolution_add_fusion.2
  338.1 3.4 convolution_add_fusion.2
  344.6 3.4 convolution_add_fusion.2
  351.2 3.4 convolution_add_fusion.2
  357.7 3.4 convolution_add_fusion.2
  364.2 3.4 convolution_add_fusion.2
  370.8 3.4 convolution_add_fusion.2
  377.3 3.4 convolution_add_fusion.2
  383.8 3.4 convolution_add_fusion.2
  390.4 3.4 convolution_add_fusion.2
  396.9 3.4 convolution_add_fusion.2
  403.5 3.4 convolution_add_fusion.2
  410.0 3.4 convolution_add_fusion.2
  429.6 3.4 convolution_add_fusion.2
  441.6 4.7 fusion.9
  450.5 106.1 %all-reduce.2.cloned.1.call-done = f32[512,512]{1,0:T(8,128)} async-done(((f32[512,512]{1,0:T(8,128)}), f32[512,512]{1,0:T(8,128)}) %all-reduce.2.cloned.1.call-update) | async-done | bytes 1048592 | tf_op jit(solution)/shard_map/psum | solution.py:63
  (49 shorter events, 115.3 us)
Async XLA Ops:
  7.2 439.2 %copy-start = (f32[512,512]{1,0:T(8,128)S(1)}, f32[512,512]{1,0:T(8,128)}, u32[]{:S(2)}) copy-start(f32[512,512]{1,0:T(8,128)} %param.7) | copy-start | bytes 3145732
  7.2 432.6 %copy-start.1 = (f32[1,512,512]{2,1,0:T(8,128)S(1)}, f32[1,512,512]{2,1,0:T(8,128)}, u32[]{:S(2)}) copy-start(f32[1,512,512]{2,1,0:T(8,128)} %param.5) | copy-start | bytes 3145732
  7.2 120.7 %all-gather.3.cloned.1.call-start = ((), (), s32[]{:S(2)}) async-start(), calls=%async_computation | async-start | bytes 34603008 | tf_op jit(solution)/shard_map/all_gather | solution.py:13
  7.9 235.5 %all-gather.5.cloned.1.call-start = ((), (), s32[]{:S(2)}) async-start(), calls=%async_computation.1 | async-start | bytes 34603008 | tf_op jit(solution)/shard_map/all_gather | solution.py:13
  8.7 547.9 %all-reduce.2.cloned.1.call-start = ((), (), s32[]{:S(2)}) async-start(), calls=%async_computation.2 | async-start | bytes 2097152 | tf_op jit(solution)/shard_map/psum | solution.py:63
Sparse Core Ops, SparseCore 0:
  10.3 117.5 all-gather.2
  130.2 113.1 all-gather.4
  449.3 107.2 all-reduce.1
where the time goes:
time: 568 us; the launch traced here: 565 us
  waiting for transfers between devices  340 us (60%)
  matrix products  204 us (36%)
  between operations  13.8 us (2%)
    all_gather x2, waiting for transfers between devices, entering(): gathered = jax.tree.map(lambda a: lax.all_gather(a, axis), part)  232 us
    dot_general x32, matrix products, product(): jnp.dot(left, right, precision=highest, preferred_element_type=jnp.float32)  110 us
    psum x1, waiting for transfers between devices, on_device(): gradient = lax.psum(accumulated, 'tm') / (total_blocks - 1)  106 us
    dot_general x31, matrix products, times_transposed(): lax.dot_general(left, right, (((1,), (1,)), ((), ())), precision=highest,...  94.5 us
  transfers between devices with their start and end apart: 3, of which 3 were waited for; matrix products, arithmetic and copies ran while one was open for 1% of the time, Pallas kernels for 0%

commit v1 on v0

--- a/solution.py
+++ b/solution.py
@@ -60,7 +60,7 @@
         jnp.float32
     )
     accumulated = current_entry * (previous_step_cross - product(transition_est, covariance))
-    gradient = lax.psum(accumulated, "tm") / (total_blocks - 1)
+    gradient = jnp.sum(lax.all_gather(accumulated, "tm"), axis=0) / (total_blocks - 1)
     cov_blocks = jnp.stack(collected[::-1], axis=0)
     return (cov_blocks, gradient)
 

time: 568 us -> 588 us (1.035)
  other arithmetic: 2.3 us -> 13.3 us
  waiting for transfers between devices: 340 us -> 349 us
    all_gather x0 -> x1, waiting for transfers between devices: none -> 116 us  [on_device(): lax.all_gather(accumulated, 'tm')]
    psum x1 -> x0, waiting for transfers between devices: 106 us -> none  [on_device(): gradient = lax.psum(accumulated, 'tm') / (total_blocks - 1)]
    reduce_sum x0 -> x1, other arithmetic: none -> 12.3 us  [on_device(): jnp.sum(lax.all_gather(accumulated, 'tm'), axis=0) / (total_blocks - 1)]
where the time goes in v1:
time: 588 us; the launch traced here: 586 us
  waiting for transfers between devices  349 us (59%)
  matrix products  204 us (35%)
  between operations  13.8 us (2%)
  other arithmetic  13.3 us (2%)
    all_gather x2, waiting for transfers between devices, entering(): gathered = jax.tree.map(lambda a: lax.all_gather(a, axis), part)  232 us
    all_gather x1, waiting for transfers between devices, on_device(): lax.all_gather(accumulated, 'tm')  116 us
    dot_general x32, matrix products, product(): jnp.dot(left, right, precision=highest, preferred_element_type=jnp.float32)  110 us
    dot_general x31, matrix products, times_transposed(): lax.dot_general(left, right, (((1,), (1,)), ((), ())), precision=highest,...  94.5 us
    reduce_sum x1, other arithmetic, on_device(): jnp.sum(lax.all_gather(accumulated, 'tm'), axis=0) / (total_blocks - 1)  12.3 us
  transfers between devices with their start and end apart: 3, of which 3 were waited for; matrix products, arithmetic and copies ran while one was open for 1% of the time, Pallas kernels for 0%

profile of v1, /device:TPU:1, one launch (start us, length us, event | category | flops | bytes accessed | tf_op | source)
XLA Modules:
  0.0 586.0 jit_solution(1464132186181531643)
XLA Ops:
  11.3 116.7 %all-gather.5.cloned.1.call-done = f32[32,512,512]{2,1,0:T(8,128)} async-done(((f32[1,512,512]{2,1,0:T(8,128)}), f32[32,512,512]{2,1,0:T(8,128)}) %all-gather.5.cloned.1.call-update) | async-done | bytes 33554448 | tf_op jit(solution)/shard_map/all_gather | solution.py:13
  127.9 115.5 %all-gather.7.cloned.1.call-done = f32[32,512,512]{2,1,0:T(8,128)} async-done(((f32[1,512,512]{2,1,0:T(8,128)}), f32[32,512,512]{2,1,0:T(8,128)}) %all-gather.7.cloned.1.call-update) | async-done | bytes 33554448 | tf_op jit(solution)/shard_map/all_gather | solution.py:13
  243.5 196.2 %while.14 = (s32[]{:T(128)}, f32[512,512]{1,0:T(8,128)S(1)}, s32[]{:T(128)}, f32[32,512,512]{2,1,0:T(8,128)}, f32[32,512,512]{2,1,0:T(8,128)}, /*index=5*/s32[]{:T(128)}, s32[]{:T(128)}, s32[]{:T(128)}, s32[]{:T(128)}) while((s32[]{:T(128)}, f32[512,512]{1,0:T(8,128)S(1)}, s32[]{:T(128)}, f32[32,512,512]{2,1,0:T(8,128)}, ...), condition=%wide.region_1.2_spmd, body=%wide.region_0.1_spmd.sunk | while | flops 3221487616 | bytes 7341199 | solution.py:22
  246.6 3.4 convolution_add_fusion.2
  253.2 3.4 convolution_add_fusion.2
  259.7 3.4 convolution_add_fusion.2
  266.2 3.4 convolution_add_fusion.2
  272.8 3.4 convolution_add_fusion.2
  279.3 3.4 convolution_add_fusion.2
  285.8 3.4 convolution_add_fusion.2
  292.4 3.4 convolution_add_fusion.2
  298.9 3.4 convolution_add_fusion.2
  305.4 3.4 convolution_add_fusion.2
  312.0 3.4 convolution_add_fusion.2
  318.5 3.4 convolution_add_fusion.2
  325.0 3.4 convolution_add_fusion.2
  331.6 3.4 convolution_add_fusion.2
  338.1 3.4 convolution_add_fusion.2
  344.6 3.4 convolution_add_fusion.2
  351.2 3.4 convolution_add_fusion.2
  357.7 3.4 convolution_add_fusion.2
  364.2 3.4 convolution_add_fusion.2
  370.8 3.4 convolution_add_fusion.2
  377.3 3.4 convolution_add_fusion.2
  383.8 3.4 convolution_add_fusion.2
  390.4 3.4 convolution_add_fusion.2
  396.9 3.4 convolution_add_fusion.2
  403.5 3.4 convolution_add_fusion.2
  429.6 3.4 convolution_add_fusion.2
  441.6 4.7 fusion.9
  450.5 115.6 %all-gather.9.cloned.1.call-done = f32[16384,512]{1,0:T(8,128)} async-done(((f32[512,512]{1,0:T(8,128)}), f32[16384,512]{1,0:T(8,128)}) %all-gather.9.cloned.1.call-update) | async-done | bytes 33554448 | tf_op jit(solution)/shard_map/all_gather | solution.py:63
  566.1 12.3 %reduce_sum.9 = f32[512,512]{1,0:T(8,128)S(1)} reduce(f32[32,512,512]{2,1,0:T(8,128)} %bitcast.42, f32[]{:T(128)} %constant.42.clone.1), dimensions={0}, to_apply=%region_2.3 | reduce | flops 8126464 | bytes 34603012 | tf_op jit(solution)/shard_map/reduce_sum | solution.py:63
  (50 shorter events, 117.5 us)
Async XLA Ops:
  7.2 439.2 %copy-start = (f32[512,512]{1,0:T(8,128)S(1)}, f32[512,512]{1,0:T(8,128)}, u32[]{:S(2)}) copy-start(f32[512,512]{1,0:T(8,128)} %param.7) | copy-start | bytes 3145732
  7.2 432.6 %copy-start.1 = (f32[1,512,512]{2,1,0:T(8,128)S(1)}, f32[1,512,512]{2,1,0:T(8,128)}, u32[]{:S(2)}) copy-start(f32[1,512,512]{2,1,0:T(8,128)} %param.5) | copy-start | bytes 3145732
  7.2 120.7 %all-gather.5.cloned.1.call-start = ((), (), s32[]{:S(2)}) async-start(), calls=%async_computation | async-start | bytes 34603008 | tf_op jit(solution)/shard_map/all_gather | solution.py:13
  7.9 235.5 %all-gather.7.cloned.1.call-start = ((), (), s32[]{:S(2)}) async-start(), calls=%async_computation.1 | async-start | bytes 34603008 | tf_op jit(solution)/shard_map/all_gather | solution.py:13
  8.7 557.4 %all-gather.9.cloned.1.call-start = ((), (), s32[]{:S(2)}) async-start(), calls=%async_computation.2 | async-start | bytes 34603008 | tf_op jit(solution)/shard_map/all_gather | solution.py:63
Sparse Core Ops, SparseCore 0:
  10.3 117.5 all-gather.4
  130.2 113.1 all-gather.6
  449.3 116.7 all-gather.8
